TPU v7x, 32 devices: a whole 2x2x4 slice. The times are simulated.
32 devices in a mesh: row: 16 (over z, y, x), col: 2 (over core).
Axes of the slice: x: 2, y: 2, z: 4, core: 2. Of those that a mesh axis runs over, the one named last changes fastest.
Arguments:
- top_tensor: bfloat16 [2304, 2304], P('row', 'col'), may hold values from -3 to 3
- bottom_tensor: bfloat16 [2304, 2304], P(('col', 'row')), may hold values from -3 to 3
- left_proj: bfloat16 [2304, 48], replicated, may hold values from -0.125 to 0.125
- right_proj: bfloat16 [2304, 48], replicated, may hold values from -0.125 to 0.125
Outputs:
- coarse: bfloat16 [2304, 2304], P(('col', 'row'))
All inputs are finite; a program needn't handle non-finite values.
Results may differ from a plain program's by a relative error of at most 0.0065.
Values may be sent and summed in bfloat16 or wider, within the bound.
A program may use at most 128 MiB of HBM per device.

v0:
```python
import jax
import jax.numpy as jnp
from jax import lax
from jax.sharding import PartitionSpec as P


def place_rows(arrived, window, rows_here, bond_dim, row_count):
    slot_ids = jnp.arange(row_count * window, dtype=jnp.int32)
    source_dev = slot_ids // window
    target_upper = source_dev * rows_here // bond_dim + slot_ids % window
    placing = (target_upper[:, None] == jnp.arange(bond_dim, dtype=jnp.int32)[None, :]).astype(
        jnp.float32
    )
    return jnp.einsum("rsb,su->rub", arrived, placing, precision=lax.Precision.HIGHEST)


def local(top_tensor, bottom_tensor, left_proj, right_proj):
    bond_dim = right_proj.shape[1]
    rows_here = top_tensor.shape[0]
    block_len = top_tensor.shape[1] // bond_dim
    lower_rows = lax.all_gather(bottom_tensor, "row", axis=0, tiled=True)
    left_table = left_proj.reshape(bond_dim, bond_dim, bond_dim)
    upper_part = top_tensor.reshape(rows_here, block_len, bond_dim)
    weighted = jnp.einsum(
        "rml,lka->ramk", upper_part, left_table, preferred_element_type=jnp.float32
    )
    weighted = weighted.astype(jnp.bfloat16).reshape(rows_here * bond_dim, block_len * bond_dim)
    window = rows_here // bond_dim + 2
    row_count = lax.axis_size("row")
    start_row = lax.axis_index("row") * rows_here
    first_upper = start_row // bond_dim
    offset_rows = start_row - first_upper * bond_dim
    group_size = 8
    groups = bond_dim // group_size
    column_sets = lower_rows.reshape(block_len * bond_dim, groups, group_size * bond_dim).transpose(
        1, 0, 2
    )

    def one_group(columns):
        product_part = jnp.dot(weighted, columns, preferred_element_type=jnp.float32).astype(
            jnp.bfloat16
        )
        product_part = product_part.reshape(rows_here, bond_dim, group_size, bond_dim)
        padded = jnp.zeros((window * bond_dim, bond_dim, group_size, bond_dim), jnp.bfloat16)
        padded = lax.dynamic_update_slice_in_dim(padded, product_part, offset_rows, 0)
        regrid = padded.reshape(window, bond_dim, bond_dim, group_size, bond_dim).transpose(
            0, 2, 3, 1, 4
        )
        regrid = regrid.reshape(window * bond_dim * group_size, bond_dim * bond_dim)
        projected = jnp.dot(regrid, right_proj, preferred_element_type=jnp.float32)
        return projected.reshape(window, bond_dim, group_size, bond_dim)

    stacked = lax.map(one_group, column_sets)
    per_down = stacked.transpose(0, 3, 2, 1, 4).reshape(bond_dim, bond_dim, window, bond_dim)
    summed = lax.psum_scatter(per_down, "col", scatter_dimension=0, tiled=True)
    summed = summed.reshape(summed.shape[0] * bond_dim, window, bond_dim)
    arrived = lax.all_to_all(summed, "row", split_axis=0, concat_axis=1, tiled=True)
    combined = place_rows(arrived, window, rows_here, bond_dim, row_count)
    out_rows = combined.shape[0]
    return combined.reshape(out_rows, bond_dim * bond_dim).astype(jnp.bfloat16)


def solution(mesh):
    return jax.shard_map(
        local,
        mesh=mesh,
        in_specs=(P("row", "col"), P(("col", "row"), None), P(), P()),
        out_specs=P(("col", "row"), None),
        check_vma=False,
    )
```

profile of v0, /device:TPU:8, one launch (start us, length us, event | category | flops | bytes accessed | tf_op | source)
XLA Modules:
  0.0 962.5 jit_solution(11929934144060463136)
XLA Ops:
  23.4 122.5 %copy.36 = bf16[144,48,24,48]{3,2,1,0:T(8,128)(2,1)} copy(bf16[144,48,24,48]{0,1,2,3:T(8,128)(2,1)} %convert_bitcast_fusion) | data formatting | bytes 31850496 | tf_op jit(solution)/shard_map/convert_element_type | solution.py:27
  145.9 52.9 %reshape.74 = bf16[6912,1152]{1,0:T(8,128)(2,1)} reshape(bf16[144,48,24,48]{3,2,1,0:T(8,128)(2,1)} %copy.36) | data formatting | bytes 31850496 | tf_op jit(solution)/shard_map/reshape | solution.py:27
  207.5 674.2 %while.12 = (s32[]{:T(128)}, f32[6,5,48,8,48]{4,2,1,3,0:T(8,128)}, bf16[6,1152,384]{1,2,0:T(8,128)(2,1)}, bf16[6912,1152]{1,0:T(8,128)(2,1)}, s32[]{:T(128)}, /*...) while((s32[]{:T(128)}, f32[6,5,48,8,48]{4,2,1,3,0:T(8,128)}, bf16[6,1152,384]{1,2,0:T(8,128)(2,1)}, ...), condition=%wide.region_1.2_spmd, body=%wide.region_0.1_spmd.sunk | while | flops 6542622720 | bytes 147924096 | solution.py:53
  207.5 16.7 %fusion.31 = bf16[6912,384]{0,1:T(8,128)(2,1)} fusion(bf16[6912,1152]{1,0:T(8,128)(2,1)} %get-tuple-element.166, bf16[6,1152,384]{1,2,0:T(8,128)(2,1)} %get-tuple-element.165, s32[]{:T(128)} %get-tuple-element.155), kind=kOutput, calls=%fused_computation.1.clone.1 | convolution fusion | flops 6117949440 | bytes 22118912 | tf_op jit(solution)/shard_map/while/body/eval_jaxpr/dot_general | solution.py:40
  232.1 19.1 %reshape.85 = bf16[144,48,8,48]{3,2,1,0:T(8,128)(2,1)} reshape(bf16[6912,384]{1,0:T(8,128)(2,1)} %copy.68) | data formatting | bytes 10616832 | tf_op jit(solution)/shard_map/while/body/eval_jaxpr/reshape | solution.py:43
  263.5 16.7 %copy.69 = bf16[5,48,8,48,48]{4,3,2,1,0:T(8,128)(2,1)} copy(bf16[5,48,8,48,48]{4,2,1,3,0:T(8,128)(2,1)S(1)} %bitcast.64) | data formatting | bytes 17694720 | tf_op jit(solution)/shard_map/while/body/eval_jaxpr/transpose | solution.py:46
  280.2 32.5 %reshape.86 = bf16[5,48,8,2304]{3,2,1,0:T(8,128)(2,1)} reshape(bf16[5,48,8,48,48]{4,3,2,1,0:T(8,128)(2,1)} %copy.69) | data formatting | bytes 17694720 | tf_op jit(solution)/shard_map/reshape.50
  319.8 16.6 %fusion.31 = bf16[6912,384]{0,1:T(8,128)(2,1)} fusion(bf16[6912,1152]{1,0:T(8,128)(2,1)} %get-tuple-element.166, bf16[6,1152,384]{1,2,0:T(8,128)(2,1)} %get-tuple-element.165, s32[]{:T(128)} %get-tuple-element.155), kind=kOutput, calls=%fused_computation.1.clone.1 | convolution fusion | flops 6117949440 | bytes 22118912 | tf_op jit(solution)/shard_map/while/body/eval_jaxpr/dot_general | solution.py:40
  344.5 19.1 %reshape.85 = bf16[144,48,8,48]{3,2,1,0:T(8,128)(2,1)} reshape(bf16[6912,384]{1,0:T(8,128)(2,1)} %copy.68) | data formatting | bytes 10616832 | tf_op jit(solution)/shard_map/while/body/eval_jaxpr/reshape | solution.py:43
  375.9 16.7 %copy.69 = bf16[5,48,8,48,48]{4,3,2,1,0:T(8,128)(2,1)} copy(bf16[5,48,8,48,48]{4,2,1,3,0:T(8,128)(2,1)S(1)} %bitcast.64) | data formatting | bytes 17694720 | tf_op jit(solution)/shard_map/while/body/eval_jaxpr/transpose | solution.py:46
  392.5 32.5 %reshape.86 = bf16[5,48,8,2304]{3,2,1,0:T(8,128)(2,1)} reshape(bf16[5,48,8,48,48]{4,3,2,1,0:T(8,128)(2,1)} %copy.69) | data formatting | bytes 17694720 | tf_op jit(solution)/shard_map/reshape.50
  456.8 19.1 %reshape.85 = bf16[144,48,8,48]{3,2,1,0:T(8,128)(2,1)} reshape(bf16[6912,384]{1,0:T(8,128)(2,1)} %copy.68) | data formatting | bytes 10616832 | tf_op jit(solution)/shard_map/while/body/eval_jaxpr/reshape | solution.py:43
  488.2 16.7 %copy.69 = bf16[5,48,8,48,48]{4,3,2,1,0:T(8,128)(2,1)} copy(bf16[5,48,8,48,48]{4,2,1,3,0:T(8,128)(2,1)S(1)} %bitcast.64) | data formatting | bytes 17694720 | tf_op jit(solution)/shard_map/while/body/eval_jaxpr/transpose | solution.py:46
  504.9 32.5 %reshape.86 = bf16[5,48,8,2304]{3,2,1,0:T(8,128)(2,1)} reshape(bf16[5,48,8,48,48]{4,3,2,1,0:T(8,128)(2,1)} %copy.69) | data formatting | bytes 17694720 | tf_op jit(solution)/shard_map/reshape.50
  569.1 19.1 %reshape.85 = bf16[144,48,8,48]{3,2,1,0:T(8,128)(2,1)} reshape(bf16[6912,384]{1,0:T(8,128)(2,1)} %copy.68) | data formatting | bytes 10616832 | tf_op jit(solution)/shard_map/while/body/eval_jaxpr/reshape | solution.py:43
  600.5 16.7 %copy.69 = bf16[5,48,8,48,48]{4,3,2,1,0:T(8,128)(2,1)} copy(bf16[5,48,8,48,48]{4,2,1,3,0:T(8,128)(2,1)S(1)} %bitcast.64) | data formatting | bytes 17694720 | tf_op jit(solution)/shard_map/while/body/eval_jaxpr/transpose | solution.py:46
  617.2 32.5 %reshape.86 = bf16[5,48,8,2304]{3,2,1,0:T(8,128)(2,1)} reshape(bf16[5,48,8,48,48]{4,3,2,1,0:T(8,128)(2,1)} %copy.69) | data formatting | bytes 17694720 | tf_op jit(solution)/shard_map/reshape.50
  681.5 19.1 %reshape.85 = bf16[144,48,8,48]{3,2,1,0:T(8,128)(2,1)} reshape(bf16[6912,384]{1,0:T(8,128)(2,1)} %copy.68) | data formatting | bytes 10616832 | tf_op jit(solution)/shard_map/while/body/eval_jaxpr/reshape | solution.py:43
  712.9 16.7 %copy.69 = bf16[5,48,8,48,48]{4,3,2,1,0:T(8,128)(2,1)} copy(bf16[5,48,8,48,48]{4,2,1,3,0:T(8,128)(2,1)S(1)} %bitcast.64) | data formatting | bytes 17694720 | tf_op jit(solution)/shard_map/while/body/eval_jaxpr/transpose | solution.py:46
  729.5 32.5 %reshape.86 = bf16[5,48,8,2304]{3,2,1,0:T(8,128)(2,1)} reshape(bf16[5,48,8,48,48]{4,3,2,1,0:T(8,128)(2,1)} %copy.69) | data formatting | bytes 17694720 | tf_op jit(solution)/shard_map/reshape.50
  793.9 19.1 %reshape.85 = bf16[144,48,8,48]{3,2,1,0:T(8,128)(2,1)} reshape(bf16[6912,384]{1,0:T(8,128)(2,1)} %copy.68) | data formatting | bytes 10616832 | tf_op jit(solution)/shard_map/while/body/eval_jaxpr/reshape | solution.py:43
  825.3 16.7 %copy.69 = bf16[5,48,8,48,48]{4,3,2,1,0:T(8,128)(2,1)} copy(bf16[5,48,8,48,48]{4,2,1,3,0:T(8,128)(2,1)S(1)} %bitcast.64) | data formatting | bytes 17694720 | tf_op jit(solution)/shard_map/while/body/eval_jaxpr/transpose | solution.py:46
  841.9 32.5 %reshape.86 = bf16[5,48,8,2304]{3,2,1,0:T(8,128)(2,1)} reshape(bf16[5,48,8,48,48]{4,3,2,1,0:T(8,128)(2,1)} %copy.69) | data formatting | bytes 17694720 | tf_op jit(solution)/shard_map/reshape.50
  914.6 27.0 %all-to-all-done = f32[16,1,17280]{2,1,0:T(1,128)S(1)} async-done(((f32[16,1,17280]{2,1,0:T(1,128)}), f32[16,1,17280]{2,1,0:T(1,128)S(1)}, u32[]{:S(2)}, u32[]{:S(2)}) %all-to-all-start) | async-done | bytes 1105952 | tf_op jit(solution)/shard_map/all_to_all | solution.py:57
  (71 shorter events, 303.8 us)
Async XLA Ops:
  6.5 192.3 %all-gather.2.cloned.1.call-start = ((), (), s32[]{:S(2)}) async-start(), calls=%async_computation.2 | async-start | bytes 5640192 | tf_op jit(solution)/shard_map/all_gather | solution.py:21
  7.3 890.4 %reduce-scatter.2.cloned.1.call-start = ((), (), s32[]{:S(2)}) async-start(), calls=%async_computation.3 | async-start | bytes 8847360 | tf_op jit(solution)/shard_map/reduce_scatter | solution.py:55
  198.8 8.6 copy-start.1
  251.2 5.0 copy-start
  363.6 5.0 copy-start
  475.9 5.0 copy-start
  588.2 5.0 copy-start
  700.6 5.0 copy-start
  812.9 5.0 copy-start
  908.2 33.3 %all-to-all-start = ((f32[16,1,17280]{2,1,0:T(1,128)}), f32[16,1,17280]{2,1,0:T(1,128)S(1)}, u32[]{:S(2)}, u32[]{:S(2)}) async-start(f32[16,1,17280]{2,1,0:T(1,128)} %reshape.81), calls=%async_computation.1 | async-start | bytes 2211840 | tf_op jit(solution)/shard_map/all_to_all | solution.py:57
Sparse Core Ops, SparseCore 0:
  10.1 86.2 all-gather.1
  881.8 15.8 reduce-scatter.1
where the time goes:
time: 973 us; the launch traced here: 962 us
  local copies, waits for them, and re-layouts  745 us (77%)
  matrix products  150 us (15%)
  waiting for transfers between devices  43.8 us (5%)
  between operations  13.5 us (1%)
    another operation x12, local copies, waits for them, and re-layouts  224 us
    convert_element_type x1, local copies, waits for them, and re-layouts, local(): weighted.astype(jnp.bfloat16)  123 us
    reshape x6, local copies, waits for them, and re-layouts, one_group(): product_part.reshape(rows_here, bond_dim, group_size, bond_dim)  114 us
    transpose x6, local copies, waits for them, and re-layouts, one_group(): padded.reshape(window, bond_dim, bond_dim, group_size, bond_dim)  100 us
    dot_general x6, matrix products, one_group(): jnp.dot(weighted, columns, preferred_element_type=jnp.float32)  99.9 us
    reshape x1, local copies, waits for them, and re-layouts, local(): weighted.astype(jnp.bfloat16)  52.9 us
    convert_element_type x6, local copies, waits for them, and re-layouts, one_group(): jnp.dot(weighted, columns, preferred_element_type=jnp.float32)  48.2 us
    dynamic_update_slice x6, local copies, waits for them, and re-layouts, one_group(): lax.dynamic_update_slice_in_dim(padded, product_part, offset_rows, 0)  43.7 us
  transfers between devices with their start and end apart: 3, of which 2 were waited for; matrix products, arithmetic and copies ran while one was open for 20% of the time, Pallas kernels for 0%

commit v1 on v0

--- a/solution.py
+++ b/solution.py
@@ -1,6 +1,8 @@
 import jax
 import jax.numpy as jnp
 from jax import lax
+from jax.experimental import pallas as pl
+from jax.experimental.pallas import tpu as pltpu
 from jax.sharding import PartitionSpec as P
 
 
@@ -14,7 +16,7 @@
     return jnp.einsum("rsb,su->rub", arrived, placing, precision=lax.Precision.HIGHEST)
 
 
-def local(top_tensor, bottom_tensor, left_proj, right_proj):
+def local_windowed(top_tensor, bottom_tensor, left_proj, right_proj):
     bond_dim = right_proj.shape[1]
     rows_here = top_tensor.shape[0]
     block_len = top_tensor.shape[1] // bond_dim
@@ -60,6 +62,163 @@
     return combined.reshape(out_rows, bond_dim * bond_dim).astype(jnp.bfloat16)
 
 
+TILE = 256
+CHUNKS = 2
+VMEM_LIMIT = 60 * 1024 * 1024
+
+
+def tiled_blocks(proj, group):
+    lanes = group * proj.shape[2]
+    pad = jnp.zeros(proj.shape[:2] + (TILE - lanes,), proj.dtype)
+    return jnp.concatenate([proj] * group + [pad], axis=2)
+
+
+def block_diagonal(tiled, group):
+    size = tiled.shape[0]
+    lane_block = lax.broadcasted_iota(jnp.int32, tiled.shape, 1) // size
+    zero = jnp.zeros_like(tiled)
+    rows = [jnp.where(lane_block == k, tiled, zero) for k in range(group)]
+    rows.append(jnp.zeros((TILE - group * size, TILE), tiled.dtype))
+    return jnp.concatenate(rows, axis=0)
+
+
+def weight_upper(upper_part, left_tiled, bond_dim, ups, group):
+    rows, padded = upper_part.shape
+    tiles = padded // TILE
+    out_rows = ups * bond_dim
+    halves = TILE // 128
+
+    def body(upper_ref, left_ref, out_ref, scratch):
+        def one_left(a, carry):
+            weights = block_diagonal(left_ref[a], group)
+            part = jnp.dot(upper_ref[...], weights, preferred_element_type=jnp.float32)
+            for up in range(ups):
+                for h in range(halves):
+                    scratch.at[h][pl.ds(up * bond_dim + a, bond_dim, stride=out_rows), :] = part[
+                        up * bond_dim : (up + 1) * bond_dim, h * 128 : (h + 1) * 128
+                    ]
+            return carry
+
+        lax.fori_loop(0, bond_dim, one_left, 0, unroll=4)
+        for h in range(halves):
+            out_ref[:, :, h * 128 : (h + 1) * 128] = (
+                scratch[h].astype(jnp.bfloat16).reshape(bond_dim, out_rows, 128)
+            )
+
+    return pl.pallas_call(
+        body,
+        grid=(tiles,),
+        in_specs=[
+            pl.BlockSpec((rows, TILE), lambda t: (0, t)),
+            pl.BlockSpec(left_tiled.shape, lambda t: (0, 0, 0)),
+        ],
+        out_specs=pl.BlockSpec((bond_dim, out_rows, TILE), lambda t: (0, 0, t)),
+        out_shape=jax.ShapeDtypeStruct((bond_dim, out_rows, padded), jnp.bfloat16),
+        scratch_shapes=[pltpu.VMEM((halves, bond_dim * out_rows, 128), jnp.float32)],
+        compiler_params=pltpu.CompilerParams(vmem_limit_bytes=VMEM_LIMIT),
+        name="weight_upper",
+    )(upper_part, left_tiled)
+
+
+def contract(weighted, lower, right_tiled, bond_dim, group, step):
+    out_rows, padded = weighted.shape[1:]
+    in_rows, in_cols = lower.shape
+    span = group * bond_dim
+    row_tiles = padded // TILE
+    col_tiles = -(-in_cols // span)
+    steps = bond_dim // step
+
+    def body(w_ref, lower_ref, right_ref, out_ref, lower_pad, acc):
+        @pl.when(pl.program_id(0) == 0)
+        def _():
+            lower_pad[...] = jnp.zeros_like(lower_pad)
+            acc[...] = jnp.zeros_like(acc)
+            for i in range(row_tiles):
+                height = min(span, in_rows - i * span)
+                for j in range(col_tiles):
+                    width = min(span, in_cols - j * span)
+                    lower_pad[i * TILE : i * TILE + height, j * TILE : j * TILE + width] = lower_ref[
+                        i * span : i * span + height, j * span : j * span + width
+                    ]
+
+        weights = jnp.concatenate(
+            [block_diagonal(right_ref[k], group) for k in range(step)], axis=0
+        )
+        left = w_ref[...].reshape(step * out_rows, padded)
+        for j in range(col_tiles):
+            cols = slice(j * TILE, (j + 1) * TILE)
+            paired = jnp.dot(left, lower_pad[:, cols], preferred_element_type=jnp.float32)
+            paired = paired.astype(jnp.bfloat16)
+            wide = jnp.concatenate(
+                [paired[k * out_rows : (k + 1) * out_rows] for k in range(step)], axis=1
+            )
+            acc[:, cols] += jnp.dot(wide, weights, preferred_element_type=jnp.float32)
+
+        @pl.when(pl.program_id(0) == steps - 1)
+        def _():
+            for j in range(col_tiles):
+                width = min(span, in_cols - j * span)
+                out_ref[:, j * span : j * span + width] = acc[
+                    :, j * TILE : j * TILE + width
+                ].astype(jnp.bfloat16)
+
+    return pl.pallas_call(
+        body,
+        grid=(steps,),
+        in_specs=[
+            pl.BlockSpec((step, out_rows, padded), lambda r: (r, 0, 0)),
+            pl.BlockSpec((in_rows, in_cols), lambda r: (0, 0)),
+            pl.BlockSpec((step, bond_dim, TILE), lambda r: (r, 0, 0)),
+        ],
+        out_specs=pl.BlockSpec((out_rows, in_cols), lambda r: (0, 0)),
+        out_shape=jax.ShapeDtypeStruct((out_rows, in_cols), jnp.bfloat16),
+        scratch_shapes=[
+            pltpu.VMEM((padded, col_tiles * TILE), jnp.bfloat16),
+            pltpu.VMEM((out_rows, col_tiles * TILE), jnp.float32),
+        ],
+        compiler_params=pltpu.CompilerParams(vmem_limit_bytes=VMEM_LIMIT),
+        name="contract",
+    )(weighted, lower, right_tiled)
+
+
+def local(top_tensor, bottom_tensor, left_proj, right_proj):
+    bond_dim = right_proj.shape[1]
+    rows_here = top_tensor.shape[0]
+    if rows_here % bond_dim or bond_dim % 16 or bond_dim > TILE:
+        return local_windowed(top_tensor, bottom_tensor, left_proj, right_proj)
+    block_len = top_tensor.shape[1] // bond_dim
+    ups = rows_here // bond_dim
+    group = TILE // bond_dim
+    chunk_cols = bottom_tensor.shape[1] // CHUNKS
+    lowers = [
+        lax.all_gather(
+            bottom_tensor[:, c * chunk_cols : (c + 1) * chunk_cols], "row", axis=0, tiled=True
+        )
+        for c in range(CHUNKS)
+    ]
+    left_tiled = tiled_blocks(
+        left_proj.reshape(bond_dim, bond_dim, bond_dim).transpose(2, 0, 1), group
+    )
+    right_tiled = tiled_blocks(right_proj.reshape(bond_dim, bond_dim, bond_dim), group)
+    tiles = -(-block_len // group)
+    span = group * bond_dim
+    upper_part = jnp.pad(top_tensor, ((0, 0), (0, tiles * span - top_tensor.shape[1])))
+    upper_part = jnp.pad(
+        upper_part.reshape(rows_here, tiles, span), ((0, 0), (0, 0), (0, TILE - span))
+    ).reshape(rows_here, tiles * TILE)
+    weighted = weight_upper(upper_part, left_tiled, bond_dim, ups, group)
+    step = 4
+    parts = [contract(weighted, lower, right_tiled, bond_dim, group, step) for lower in lowers]
+    partial = jnp.concatenate(parts, axis=1).reshape(ups, bond_dim, bond_dim, bond_dim)
+    partial = partial.transpose(2, 1, 0, 3).reshape(bond_dim * bond_dim, ups * bond_dim)
+    arrived = lax.all_to_all(partial, ("col", "row"), split_axis=0, concat_axis=0, tiled=True)
+    cols, row_count = lax.axis_size("col"), lax.axis_size("row")
+    out_rows = bond_dim * bond_dim // (cols * row_count)
+    arrived = arrived.reshape(cols, row_count, out_rows, ups * bond_dim)
+    combined = jnp.sum(arrived.astype(jnp.float32), axis=0).astype(jnp.bfloat16)
+    return combined.transpose(1, 0, 2).reshape(out_rows, bond_dim * bond_dim)
+
+
 def solution(mesh):
     return jax.shard_map(
         local,

time: 973 us -> 247 us (0.25)
  local copies, waits for them, and re-layouts: 745 us -> 23.2 us
  matrix products: 150 us -> 0 us
  Pallas kernels: 0 us -> 135 us
  blocking collectives: 0 us -> 32.4 us
    another operation x12 -> x1, local copies, waits for them, and re-layouts: 224 us -> 0.08 us
    convert_element_type x9 -> x0, local copies, waits for them, and re-layouts: 172 us -> none  [the longest x1 123 us: local(): weighted.astype(jnp.bfloat16)]
    reshape x10 -> x5, local copies, waits for them, and re-layouts: 175 us -> 8.38 us  [the longest x2 5.04 us: local(): jnp.concatenate(parts, axis=1).reshape(ups, bond_dim, bond_dim, bond_dim)]
    dot_general x14 -> x0, matrix products: 150 us -> none  [the longest x6 99.9 us: one_group(): jnp.dot(weighted, columns, preferred_element_type=jnp.float32)]
    pallas_call x0 -> x3, Pallas kernels: none -> 135 us  [the longest x2 109 us: contract(): pl.pallas_call(body, grid=(steps,), in_specs=[pl.BlockSpec((step, out_row...]
    transpose x6 -> x0, local copies, waits for them, and re-layouts: 100 us -> none  [one_group(): padded.reshape(window, bond_dim, bond_dim, group_size, bond_dim)]
    dynamic_update_slice x12 -> x0, local copies, waits for them, and re-layouts: 50.7 us -> none  [the longest x6 43.7 us: one_group(): lax.dynamic_update_slice_in_dim(padded, product_part, offset_rows, 0)]
    all_gather x1 -> x2, waiting for transfers between devices: 0.01 us -> 37.3 us  [local(): lax.all_gather(bottom_tensor[:, c * chunk_cols:(c + 1) * chunk_cols], 'ro...]
  transfers between devices with their start and end apart: 3 -> 2, of which waited for: 2 -> 2; matrix products, arithmetic and copies ran while one was open for 20% -> 6% of each run, Pallas kernels for 0% -> 33%
where the time goes in v1:
time: 247 us; the launch traced here: 244 us
  Pallas kernels  135 us (55%)
  waiting for transfers between devices  38 us (15%)
  blocking collectives  32.4 us (13%)
  local copies, waits for them, and re-layouts  23.2 us (9%)
  between operations  13.5 us (5%)
    pallas_call x2, Pallas kernels, contract(): pl.pallas_call(body, grid=(steps,), in_specs=[pl.BlockSpec((step, out_row...  109 us
    all_gather x2, waiting for transfers between devices, local(): lax.all_gather(bottom_tensor[:, c * chunk_cols:(c + 1) * chunk_cols], 'ro...  37.3 us
    all_to_all x1, blocking collectives, local(): lax.all_to_all(partial, ('col', 'row'), split_axis=0, concat_axis=0, tile...  32.4 us
    pallas_call x1, Pallas kernels, weight_upper(): pl.pallas_call(body, grid=(tiles,), in_specs=[pl.BlockSpec((rows, TILE),...  26.2 us
    concatenate x2, local copies, waits for them, and re-layouts, tiled_blocks(): return jnp.concatenate([proj] * group + [pad], axis=2)  10.2 us
    reshape x2, local copies, waits for them, and re-layouts, local(): jnp.concatenate(parts, axis=1).reshape(ups, bond_dim, bond_dim, bond_dim)  5.04 us
  transfers between devices with their start and end apart: 2, of which 2 were waited for; matrix products, arithmetic and copies ran while one was open for 6% of the time, Pallas kernels for 33%

profile of v1, /device:TPU:8, one launch (start us, length us, event | category | flops | bytes accessed | tf_op | source)
XLA Modules:
  0.0 243.7 jit_solution(16319034611008652984)
XLA Ops:
  6.5 1.8 fusion
  8.4 0.0 all-gather.5.cloned.1.call-start
  8.4 0.7 all-gather.5.cloned.1.call-update
  9.1 1.7 reshape.28
  10.9 0.6 reshape.26
  11.6 0.1 pad.9
  11.7 0.8 copy.20
  12.5 0.3 copy.12
  12.9 0.1 broadcast.7
  12.9 5.1 %concatenate.9.left_ref = bf16[48,48,256]{2,1,0:T(8,128)(2,1)} concatenate(bf16[48,48,48]{2,1,0:T(8,128)(2,1)S(1)} %bitcast.16, bf16[48,48,48]{2,1,0:T(8,128)(2,1)S(1)} %bitcast.17, bf16[48,48,48]{2,1,0:T(8,128)(2,1)S(1)} %bitcast.18, bf16[48,48,48]{2,1,0:T(8,128)(2,1)S(1)} %bitcast.19, bf16[48,48,48]{2,1,0:T(8,128)(2,1)S(1)} %bitcast.20, bf16[48,48,16]{2,1,0:T(8,128)(2,1)S(1)} %broadcast.7), dimensions={2} | concatenate | bytes 2359296 | tf_op jit(solution)/shard_map/concatenate | solution.py:73
  18.0 5.1 %concatenate.10.right_ref = bf16[48,48,256]{2,1,0:T(8,128)(2,1)} concatenate(bf16[48,48,48]{2,1,0:T(8,128)(2,1)S(1)} %bitcast.21, bf16[48,48,48]{2,1,0:T(8,128)(2,1)S(1)} %bitcast.22, bf16[48,48,48]{2,1,0:T(8,128)(2,1)S(1)} %bitcast.23, bf16[48,48,48]{2,1,0:T(8,128)(2,1)S(1)} %bitcast.24, bf16[48,48,48]{2,1,0:T(8,128)(2,1)S(1)} %bitcast.25, bf16[48,48,16]{2,1,0:T(8,128)(2,1)S(1)} %broadcast.7), dimensions={2} | concatenate | bytes 2359296 | tf_op jit(solution)/shard_map/concatenate | solution.py:73
  23.1 26.2 %weight_upper.1.w_ref = bf16[48,144,1280]{2,1,0:T(8,128)(2,1)} custom-call(bf16[144,1280]{1,0:T(8,128)(2,1)} %bitcast.30, bf16[48,48,256]{2,1,0:T(8,128)(2,1)} %concatenate.9.left_ref), custom_call_target="tpu_custom_call" | custom-call | tf_op jit(solution)/shard_map/weight_upper/pallas_call | solution.py:108
  49.3 26.2 %all-gather.3.cloned.1.call-done.lower_ref = bf16[1152,1152]{1,0:T(8,128)(2,1)} async-done(((bf16[72,1152]{1,0:T(8,128)(2,1)}), bf16[1152,1152]{1,0:T(8,128)(2,1)}) %all-gather.3.cloned.1.call-update) | async-done | bytes 2654224 | tf_op jit(solution)/shard_map/all_gather | solution.py:194
  75.6 54.4 %contract.2 = bf16[144,1152]{1,0:T(8,128)(2,1)} custom-call(bf16[48,144,1280]{2,1,0:T(8,128)(2,1)} %weight_upper.1.w_ref, bf16[1152,1152]{1,0:T(8,128)(2,1)} %all-gather.3.cloned.1.call-done.lower_ref, bf16[48,48,256]{2,1,0:T(8,128)(2,1)} %concatenate.10.right_ref), custom_call_target="tpu_custom_call" | custom-call | tf_op jit(solution)/shard_map/contract/pallas_call | solution.py:165
  130.0 11.1 %all-gather.5.cloned.1.call-done.lower_ref = bf16[1152,1152]{1,0:T(8,128)(2,1)} async-done(((bf16[72,1152]{1,0:T(8,128)(2,1)}), bf16[1152,1152]{1,0:T(8,128)(2,1)}) %all-gather.5.cloned.1.call-update) | async-done | bytes 2654224 | tf_op jit(solution)/shard_map/all_gather | solution.py:194
  141.1 54.4 %contract.3 = bf16[144,1152]{1,0:T(8,128)(2,1)} custom-call(bf16[48,144,1280]{2,1,0:T(8,128)(2,1)} %weight_upper.1.w_ref, bf16[1152,1152]{1,0:T(8,128)(2,1)} %all-gather.5.cloned.1.call-done.lower_ref, bf16[48,48,256]{2,1,0:T(8,128)(2,1)} %concatenate.10.right_ref), custom_call_target="tpu_custom_call" | custom-call | tf_op jit(solution)/shard_map/contract/pallas_call | solution.py:165
  195.5 1.0 pad_maximum_fusion
  196.5 2.5 %reshape.30 = bf16[3,48,48,48]{3,2,1,0:T(8,128)(2,1)S(1)} reshape(bf16[144,2304]{1,0:T(8,128)(2,1)S(1)} %pad_maximum_fusion) | data formatting | bytes 1327104 | tf_op jit(solution)/shard_map/reshape | solution.py:212
  199.0 2.6 %copy.13 = bf16[3,48,48,48]{1,2,3,0:T(8,128)(2,1)S(1)} copy(bf16[3,48,48,48]{3,2,1,0:T(8,128)(2,1)S(1)} %reshape.30) | data formatting | bytes 1327104 | tf_op jit(solution)/shard_map/reshape | solution.py:212
  201.6 1.0 all_to_all.6
  202.6 0.5 copy.14
  203.1 32.4 %all_to_all.9 = bf16[32,72,144]{1,2,0:T(8,128)(2,1)S(1)} all-to-all(bf16[32,72,144]{1,2,0:T(8,128)(2,1)S(1)} %copy.14), channel_id=1, replica_groups=mesh['row'=16,'col'=2] {'col','row'}, dimensions={0} | all-to-all | bytes 1327104 | tf_op jit(solution)/shard_map/all_to_all | solution.py:214
  235.5 0.4 reduce_sum.12
  235.9 1.0 copy.19
  (9 shorter events, 0.1 us)
Async XLA Ops:
  6.5 4.3 %copy-start.1 = (bf16[144,1152]{1,0:T(8,128)(2,1)S(1)}, bf16[144,1152]{1,0:T(8,128)(2,1)}, u32[]{:S(2)}) copy-start(bf16[144,1152]{1,0:T(8,128)(2,1)} %param.4) | copy-start | bytes 995332
  6.5 69.0 %all-gather.3.cloned.1.call-start = ((), (), s32[]{:S(2)}) async-start(), calls=%async_computation.1 | async-start | bytes 2820096 | tf_op jit(solution)/shard_map/all_gather | solution.py:194
  8.4 132.7 %all-gather.5.cloned.1.call-start = ((), (), s32[]{:S(2)}) async-start(), calls=%async_computation.2 | async-start | bytes 2820096 | tf_op jit(solution)/shard_map/all_gather | solution.py:194
  10.9 1.6 copy-start.2
  130.0 65.5 %copy-start = (bf16[144,1152]{1,0:T(8,128)(2,1)S(1)}, bf16[144,1152]{1,0:T(8,128)(2,1)}, u32[]{:S(2)}) copy-start(bf16[144,1152]{1,0:T(8,128)(2,1)} %contract.2) | copy-start | bytes 995332
Sparse Core Ops, SparseCore 0:
  10.0 65.4 all-gather.2
  78.3 62.7 all-gather.4
